TPU v7x, 128 devices: a whole 4x4x4 slice. The times are simulated.
128 devices in a mesh: span: 16 (over z, y_hi, core), group: 8 (over y_lo, x).
Axes of the slice: x: 4, y: 4 (y_hi: 2, y_lo: 2; y = y_hi * 2 + y_lo), z: 4, core: 2. Of those that a mesh axis runs over, the one named last changes fastest.
Arguments:
- air_temp: float32 [8, 256, 8192], P('group', 'span'), may hold values from -6 to 6
- air_vel: float32 [8, 256, 8192], P('group', 'span'), may hold values from -0.3 to 0.3
- air_kappa: float32 [8, 256, 8192], P('group', 'span'), may hold values from 0.02 to 0.2
- group_width: int32 [8], P('group'), may hold values from 2048 to 8192
- sub_temp: float32 [16384, 64], P(('span', 'group')), may hold values from -6 to 6
- sub_coupling: bfloat16 [16384, 4, 4096], P(('span', 'group')), may hold values from -0.1875 to 0.1875
- neighbors: int32 [16384, 4], P(('span', 'group')), may hold values from 0 to 16383, as said below
- iface_count: int32 [128], P(('span', 'group')), may hold values from 768 to 1024
- iface_seg: int32 [131072], P(('span', 'group')), may hold values from 0 to 2047, as said below
- iface_owner: int32 [131072, 1], P(('span', 'group')), may hold values from 0 to 127; in each aligned block of 1024 rows (0 to 1023, 1024 to 2047, ...) at most 16 rows name the same one
- iface_block: int32 [131072], P(('span', 'group')), may hold values from 0 to 127
Outputs:
- air_out: float32 [8, 256, 8192], P('group', 'span')
- sub_out: float32 [16384, 64], P(('span', 'group'))
Inputs may be any that keep to these rules, and one draw needn't show every extreme that they name: `neighbors`: the first coupled block of every block is itself; the others lie on the same device or the one just before or after it along span+group (no wrap). `iface_seg`: the segments of one device's rows are all different. `iface_owner`: among the rows of one device no owner is named more than 16 times. `iface_count`: the live rows of a device are its first ones.
All inputs are finite; a program needn't handle non-finite values.
Results may differ from a plain program's by a relative error of at most 0.0016.
Values may be sent and summed in bfloat16 or wider, within the bound.
A program may use at most 64 MiB of HBM per device.

v0:
```python
import jax
import jax.numpy as jnp
from jax import lax
from jax.sharding import PartitionSpec as P

STEPS = 4
SSTEPS = 2
NODES = 64


uptake = 0.3
release = 0.5


def with_halo(block, sides, width, periodic):
    for axis, dim in sides:
        count = lax.axis_size(axis)
        forward = [(i, i + 1) for i in range(count - 1)]
        if periodic:
            forward.append((count - 1, 0))
        backward = [(target, source) for source, target in forward]
        low = lax.ppermute(
            lax.slice_in_dim(block, block.shape[dim] - width, None, axis=dim), axis, forward
        )
        high = lax.ppermute(lax.slice_in_dim(block, 0, width, axis=dim), axis, backward)
        block = jnp.concatenate([low, block, high], axis=dim)
    return block


def advance(padded, vel, kappa, live):
    centre = padded[:, 1:-1]
    east = padded[:, 2:]
    west = padded[:, :-2]
    north = jnp.concatenate([centre[:, :, 1:], centre[:, :, -1:]], axis=2)
    south = jnp.concatenate([centre[:, :, :1], centre[:, :, :-1]], axis=2)
    fresh = (
        centre
        + kappa * (east + west - 2.0 * centre)
        + kappa * (north + south - 2.0 * centre)
        - 0.5 * vel * (east - west)
    )
    return jnp.where(live, fresh, centre)


def per_device(
    air_temp,
    air_vel,
    air_kappa,
    group_width,
    sub_temp,
    sub_coupling,
    neighbors,
    iface_count,
    iface_seg,
    iface_owner,
    iface_block,
):
    width = air_temp.shape[2]
    live = (jnp.arange(width, dtype=jnp.int32) < group_width[0])[None, None, :]
    field = air_temp
    for step in range(STEPS):
        padded = with_halo(field, (("span", 1),), 1, True)
        field = advance(padded, air_vel, air_kappa, live)
    devices = lax.axis_size(("span", "group"))
    groups = lax.axis_size("group")
    here = lax.axis_index("span") * groups + lax.axis_index("group")
    irows = iface_seg.shape[0]
    capacity = max(2, 2 * irows // devices)
    per_line = width // NODES
    line_index = (iface_seg // per_line)[:, None]
    column_index = (iface_seg % per_line * NODES)[:, None] + jnp.arange(NODES, dtype=jnp.int32)[
        None, :
    ]
    air_rows = air_temp[0, line_index, column_index]
    owner = iface_owner[:, 0]
    active = jnp.arange(irows, dtype=jnp.int32) < iface_count[0]
    onehot = (owner[:, None] == jnp.arange(devices, dtype=jnp.int32)[None, :]).astype(jnp.int32)
    slot = jnp.sum((jnp.cumsum(onehot, axis=0) - onehot) * onehot, axis=1)
    place = owner * capacity + slot
    send_rows = (
        jnp.zeros((devices * capacity, NODES), jnp.float32)
        .at[place]
        .set(jnp.where(active[:, None], air_rows, jnp.float32(0.0)))
    )
    send_index = (
        jnp.full((devices * capacity,), -1, jnp.int32)
        .at[place]
        .set(jnp.where(active, iface_block, -1))
    )
    recv_rows = lax.all_to_all(
        send_rows, ("span", "group"), split_axis=0, concat_axis=0, tiled=True
    )
    recv_index = lax.all_to_all(
        send_index, ("span", "group"), split_axis=0, concat_axis=0, tiled=True
    )
    valid = recv_index >= 0
    target = jnp.maximum(recv_index, 0)
    gain = jnp.where(valid[:, None], uptake * (recv_rows - sub_temp[target]), jnp.float32(0.0))
    substrate = sub_temp.at[target].add(gain)
    blocks = substrate.shape[0]
    links_count = sub_coupling.shape[1]
    coupling = sub_coupling.reshape(blocks, links_count, NODES, NODES)
    local_links = neighbors - (here - 1) * blocks
    for step in range(SSTEPS):
        rounded = substrate.astype(jnp.bfloat16)
        beside_all = with_halo(rounded, ((("span", "group"), 0),), blocks, False)
        near = beside_all[local_links]
        substrate = substrate + jnp.einsum(
            "bkij,bkj->bi", coupling, near, preferred_element_type=jnp.float32
        )
    reply = substrate[target]
    returned = lax.all_to_all(reply, ("span", "group"), split_axis=0, concat_axis=0, tiled=True)
    surface = returned[place]
    delta = jnp.where(active[:, None], release * (surface - air_rows), jnp.float32(0.0))
    final = field.at[0, line_index, column_index].add(delta)
    return (final, substrate)


def solution(mesh):
    placed = (
        P("group", "span", None),
        P("group", "span", None),
        P("group", "span", None),
        P("group"),
        P(("span", "group"), None),
        P(("span", "group"), None, None),
        P(("span", "group"), None),
        P(("span", "group")),
        P(("span", "group")),
        P(("span", "group"), None),
        P(("span", "group")),
    )
    return jax.shard_map(
        per_device,
        mesh=mesh,
        in_specs=placed,
        out_specs=(P("group", "span", None), P(("span", "group"), None)),
        check_vma=False,
    )
```

profile of v0, /device:TPU:1, one launch (start us, length us, event | category | flops | bytes accessed | tf_op | source)
XLA Modules:
  0.0 1164.3 jit_solution(18206604063569723742)
XLA Ops:
  5.0 4.3 scatter_custom_fusion
  10.0 12.0 %all-to-all-start = ((s32[128,16,1]{1,2,0:T(1,128)}), s32[128,16,1]{1,2,0:T(1,128)}, u32[]{:S(2)}, u32[]{:S(2)}) async-start(s32[128,16,1]{1,2,0:T(1,128)} %bitcast.9), calls=%async_computation | async-start | bytes 131072 | tf_op jit(solution)/shard_map/all_to_all | solution.py:93
  22.0 1.7 fusion.58
  24.8 2.1 collective-permute-start.1
  27.5 2.3 fusion.60
  38.3 518.5 %gather_fusion = f32[65536]{0:T(1024)S(1)} fusion(f32[1,16,8192]{2,1,0:T(8,128)S(1)} %copy-done, s32[65536]{0:T(1024)S(1)} %reshape.318), kind=kCustom, calls=%fused_computation | custom fusion | bytes 1310720 | tf_op jit(solution)/shard_map/gather | solution.py:74
  557.0 4.1 scatter_custom_fusion.1
  562.6 7.9 copy.30
  570.5 15.6 %copy.33 = bf16[128,4,64,64]{2,3,1,0:T(8,128)(2,1)} copy(bf16[128,4,64,64]{0,3,2,1:T(8,128)(2,1)} %bitcast.51) | data formatting | bytes 8388608 | tf_op jit(solution)/shard_map/reshape | solution.py:102
  587.5 12.1 %all-to-all-start.1 = ((f32[128,1,1024]{2,1,0:T(1,128)}), f32[128,1,1024]{2,1,0:T(1,128)}, u32[]{:S(2)}, u32[]{:S(2)}) async-start(f32[128,1,1024]{2,1,0:T(1,128)} %reshape.417), calls=%async_computation.1 | async-start | bytes 1048576 | tf_op jit(solution)/shard_map/all_to_all | solution.py:90
  602.4 7.6 gather_fusion.1
  612.9 1.9 collective-permute-start.3
  616.4 2.0 collective-permute-done.3
  620.1 6.3 collective-permute-start.4
  627.1 3.0 reduce.10
  631.3 2.9 fusion.7
  634.3 11.9 %scatter_fusion = f32[128,64]{1,0:T(8,128)S(1)} fusion(f32[128,64]{1,0:T(8,128)S(1)} %copy.28, s32[2048]{0:T(1024)S(1)} %reshape.382, f32[2048,64]{1,0:T(8,128)} %fusion.7), kind=kCustom, calls=%fused_computation.8 | custom fusion | flops 131072 | bytes 1581056 | tf_op jit(solution)/shard_map/scatter-add | solution.py:99
  646.2 3.4 collective-permute-start.8
  649.6 4.3 collective-permute-start.9
  653.9 1.6 fusion.22
  656.9 4.8 fusion.38
  661.7 2.4 collective-permute-start.10
  664.1 5.5 collective-permute-start.11
  672.2 4.8 fusion.36
  677.0 5.5 gather_fusion.4
  683.9 10.6 all-to-all-start.2
  695.7 2.2 collective-permute-start.7
  698.0 2.2 collective-permute-done.6
  703.9 4.5 all-to-all-done.2
  708.5 1.9 reduce.11
  710.7 2.8 gather_fusion.5
  713.9 449.5 %scatter_fusion.1 = f32[131072]{0:T(1024)S(1)} fusion(f32[131072]{0:T(1024)S(1)} %bitcast.49, s32[65536]{0:T(1024)S(1)} %reshape.388, f32[65536]{0:T(1024)S(1)} %reshape.390), kind=kCustom, calls=%fused_computation.9 | custom fusion | flops 65536 | bytes 1048576
  (110 shorter events, 39.6 us)
Async XLA Ops:
  0.6 35.7 %copy-start.14 = (s32[3]{0:T(128)S(1)}, s32[3]{0:T(128)}, u32[]{:S(2)}) copy-start(s32[3]{0:T(128)} %constant.85) | copy-start | bytes 40
  0.6 37.7 %copy-start = (f32[1,16,8192]{2,1,0:T(8,128)S(1)}, f32[1,16,8192]{2,1,0:T(8,128)}, u32[]{:S(2)}) copy-start(f32[1,16,8192]{2,1,0:T(8,128)} %param.11) | copy-start | bytes 1572868
  3.7 28.3 %copy-start.10 = (s32[1024,1]{0,1:T(1,128)}, s32[1024,1]{0,1:T(1,128)S(1)}, u32[]{:S(2)}) copy-start(s32[1024,1]{0,1:T(1,128)S(1)} %compare_select_fusion.1) | copy-start | bytes 12292
  10.0 577.4 %all-to-all-start = ((s32[128,16,1]{1,2,0:T(1,128)}), s32[128,16,1]{1,2,0:T(1,128)}, u32[]{:S(2)}, u32[]{:S(2)}) async-start(s32[128,16,1]{1,2,0:T(1,128)} %bitcast.9), calls=%async_computation | async-start | bytes 131072 | tf_op jit(solution)/shard_map/all_to_all | solution.py:93
  23.7 586.3 %collective-permute-start = (f32[1,1,8192]{2,1,0:T(1,128)}, f32[1,1,8192]{2,1,0:T(1,128)}, u32[]{:S(2)}, u32[]{:S(2)}) collective-permute-start(f32[1,1,8192]{2,1,0:T(1,128)} %get-tuple-element.31), channel_id=1, source_target_pairs={{8,0},{16,8},{24,16},{32,24},{40,32},{48,40},{56,48},{64,56},{72,6... | collective-permute-start | bytes 98312 | tf_op jit(solution)/shard_map/ppermute | solution.py:25
  24.8 585.1 %collective-permute-start.1 = (f32[1,1,8192]{2,1,0:T(1,128)}, f32[1,1,8192]{2,1,0:T(1,128)}, u32[]{:S(2)}, u32[]{:S(2)}) collective-permute-start(f32[1,1,8192]{2,1,0:T(1,128)} %get-tuple-element.30), channel_id=1, source_target_pairs={{0,8},{8,16},{16,24},{24,32},{32,40},{40,48},{48,56},{56,64},{64,7... | collective-permute-start | bytes 98312 | tf_op jit(solution)/shard_map/ppermute | solution.py:22
  38.3 518.7 %copy-start.12 = (pred[1024]{0:T(1024)(128)(4,1)S(1)}, pred[1024]{0:T(1024)(128)(4,1)}, u32[]{:S(2)}) copy-start(pred[1024]{0:T(1024)(128)(4,1)} %iota_compare_fusion.4) | copy-start | bytes 3076
  38.3 524.2 %copy-start.9 = (f32[128,64]{0,1:T(8,128)S(1)}, f32[128,64]{0,1:T(8,128)}, u32[]{:S(2)}) copy-start(f32[128,64]{0,1:T(8,128)} %param.15) | copy-start | bytes 98308
  586.1 23.9 %copy-start.1 = (f32[1,16,8192]{2,1,0:T(8,128)S(1)}, f32[1,16,8192]{2,1,0:T(8,128)}, u32[]{:S(2)}) copy-start(f32[1,16,8192]{2,1,0:T(8,128)} %param.13) | copy-start | bytes 1572868
  586.1 23.9 %copy-start.2 = (f32[1,16,8192]{2,1,0:T(8,128)S(1)}, f32[1,16,8192]{2,1,0:T(8,128)}, u32[]{:S(2)}) copy-start(f32[1,16,8192]{2,1,0:T(8,128)} %param.12) | copy-start | bytes 1572868
  586.1 23.9 %copy-start.4 = (f32[1,16,8191]{2,1,0:T(8,128)S(1)}, f32[1,16,8191]{2,1,0:T(8,128)}, u32[]{:S(2)}) copy-start(f32[1,16,8191]{2,1,0:T(8,128)} %get-tuple-element.34) | copy-start | bytes 1572676
  586.1 23.9 %copy-start.5 = (f32[1,16,8191]{2,1,0:T(8,128)S(1)}, f32[1,16,8191]{2,1,0:T(8,128)}, u32[]{:S(2)}) copy-start(f32[1,16,8191]{2,1,0:T(8,128)} %get-tuple-element.35) | copy-start | bytes 1572676
  586.1 23.9 %copy-start.6 = (pred[8192]{0:T(1024)(128)(4,1)S(1)}, pred[8192]{0:T(1024)(128)(4,1)}, u32[]{:S(2)}) copy-start(pred[8192]{0:T(1024)(128)(4,1)} %iota_compare_fusion.3) | copy-start | bytes 24580
  587.5 39.0 %all-to-all-start.1 = ((f32[128,1,1024]{2,1,0:T(1,128)}), f32[128,1,1024]{2,1,0:T(1,128)}, u32[]{:S(2)}, u32[]{:S(2)}) async-start(f32[128,1,1024]{2,1,0:T(1,128)} %reshape.417), calls=%async_computation.1 | async-start | bytes 1048576 | tf_op jit(solution)/shard_map/all_to_all | solution.py:90
  600.7 9.4 copy-start.7
  600.7 9.4 copy-start.8
  611.5 4.9 collective-permute-start.2
  612.9 5.6 collective-permute-start.3
  620.1 33.8 %collective-permute-start.4 = (f32[1,1,8192]{2,1,0:T(1,128)S(1)}, f32[1,1,8192]{2,1,0:T(1,128)S(1)}, u32[]{:S(2)}, u32[]{:S(2)}) collective-permute-start(f32[1,1,8192]{2,1,0:T(1,128)S(1)} %get-tuple-element.19), channel_id=1, source_target_pairs={{8,0},{16,8},{24,16},{32,24},{40,32},{48,40},{56,48},{64,56},{72,6... | collective-permute-start | bytes 98312 | tf_op jit(solution)/shard_map/ppermute | solution.py:25
  626.4 27.5 %collective-permute-start.5 = (f32[1,1,8192]{2,1,0:T(1,128)S(1)}, f32[1,1,8192]{2,1,0:T(1,128)S(1)}, u32[]{:S(2)}, u32[]{:S(2)}) collective-permute-start(f32[1,1,8192]{2,1,0:T(1,128)S(1)} %get-tuple-element.18), channel_id=1, source_target_pairs={{0,8},{8,16},{16,24},{24,32},{32,40},{40,48},{48,56},{56,64},{64,7... | collective-permute-start | bytes 98312 | tf_op jit(solution)/shard_map/ppermute | solution.py:22
  634.2 21.3 %copy-start.3 = (s32[1024]{0:T(1024)S(1)}, s32[1024]{0:T(1024)}, u32[]{:S(2)}) copy-start(s32[1024]{0:T(1024)} %pad_clamp_fusion) | copy-start | bytes 12292
  646.2 9.3 collective-permute-start.8
  649.6 6.0 collective-permute-start.9
  661.7 9.0 collective-permute-start.10
  664.1 6.7 collective-permute-start.11
  677.0 33.8 %copy-start.11 = (s32[1024]{0:T(1024)S(1)}, s32[1024]{0:T(1024)}, u32[]{:S(2)}) copy-start(s32[1024]{0:T(1024)} %broadcast_clamp_fusion.1) | copy-start | bytes 12292
  682.4 31.1 %copy-start.13 = (pred[1024]{0:T(1024)(128)(4,1)S(1)}, pred[1024]{0:T(1024)(128)(4,1)}, u32[]{:S(2)}) copy-start(pred[1024]{0:T(1024)(128)(4,1)} %iota_compare_fusion.4) | copy-start | bytes 3076
  683.9 24.6 %all-to-all-start.2 = ((f32[128,1,1024]{2,1,0:T(1,128)}), f32[128,1,1024]{2,1,0:T(1,128)S(1)}, u32[]{:S(2)}, u32[]{:S(2)}) async-start(f32[128,1,1024]{2,1,0:T(1,128)} %reshape.419), calls=%async_computation.2 | async-start | bytes 1048576 | tf_op jit(solution)/shard_map/all_to_all | solution.py:112
  694.6 5.6 collective-permute-start.6
  695.7 5.8 collective-permute-start.7
where the time goes:
time: 1170 us; the launch traced here: 1160 us
  local copies, waits for them, and re-layouts  584 us (50%)
  other arithmetic  490 us (42%)
  starting transfers between devices  66.4 us (6%)
    gather x2, local copies, waits for them, and re-layouts, per_device(): air_rows = air_temp[0, line_index, column_index]  519 us
    unnamed x5, other arithmetic  453 us
  transfers between devices with their start and end apart: 15, of which 5 were waited for; matrix products, arithmetic and copies ran while one was open for 52% of the time, Pallas kernels for 0%

commit v1 on v0

--- a/solution.py
+++ b/solution.py
@@ -66,12 +66,7 @@
     here = lax.axis_index("span") * groups + lax.axis_index("group")
     irows = iface_seg.shape[0]
     capacity = max(2, 2 * irows // devices)
-    per_line = width // NODES
-    line_index = (iface_seg // per_line)[:, None]
-    column_index = (iface_seg % per_line * NODES)[:, None] + jnp.arange(NODES, dtype=jnp.int32)[
-        None, :
-    ]
-    air_rows = air_temp[0, line_index, column_index]
+    air_rows = air_temp.reshape(-1, NODES)[iface_seg]
     owner = iface_owner[:, 0]
     active = jnp.arange(irows, dtype=jnp.int32) < iface_count[0]
     onehot = (owner[:, None] == jnp.arange(devices, dtype=jnp.int32)[None, :]).astype(jnp.int32)
@@ -112,8 +107,8 @@
     returned = lax.all_to_all(reply, ("span", "group"), split_axis=0, concat_axis=0, tiled=True)
     surface = returned[place]
     delta = jnp.where(active[:, None], release * (surface - air_rows), jnp.float32(0.0))
-    final = field.at[0, line_index, column_index].add(delta)
-    return (final, substrate)
+    final = field.reshape(-1, NODES).at[iface_seg].add(delta, unique_indices=True)
+    return (final.reshape(field.shape), substrate)
 
 
 def solution(mesh):

time: 1170 us -> 202 us (0.17)
  local copies, waits for them, and re-layouts: 584 us -> 63.1 us
  other arithmetic: 490 us -> 40.5 us
    gather x3 -> x1, local copies, waits for them, and re-layouts: 521 us -> 2.81 us  [per_device(): air_rows = air_temp.reshape(-1, NODES)[iface_seg]]
    unnamed x5 -> x0, other arithmetic: 453 us -> none
  transfers between devices with their start and end apart: 15 -> 15, of which waited for: 5 -> 6; matrix products, arithmetic and copies ran while one was open for 52% -> 33% of each run, Pallas kernels for 0% -> 0%
where the time goes in v1:
time: 202 us; the launch traced here: 201 us
  starting transfers between devices  69 us (34%)
  local copies, waits for them, and re-layouts  63.1 us (31%)
  other arithmetic  40.5 us (20%)
  waiting for transfers between devices  16.5 us (8%)
  matrix products  9.54 us (5%)
  between operations  2.31 us (1%)
    ppermute x6, starting transfers between devices, with_halo(): lax.ppermute(lax.slice_in_dim(block, 0, width, axis=dim), axis, backward)  24.1 us
    reshape x1, local copies, waits for them, and re-layouts, per_device(): coupling = sub_coupling.reshape(blocks, links_count, NODES, NODES)  15.7 us
    unnamed x15, local copies, waits for them, and re-layouts  13.1 us
    ppermute x6, starting transfers between devices, with_halo(): lax.ppermute(lax.slice_in_dim(block, block.shape[dim] - width, None, axis...  12.8 us
    all_to_all x1, starting transfers between devices, per_device(): lax.all_to_all(send_rows, ('span', 'group'), split_axis=0, concat_axis=0,...  11.6 us
    scatter-add x1, other arithmetic, per_device(): substrate = sub_temp.at[target].add(gain)  11.6 us
    all_to_all x1, starting transfers between devices, per_device(): lax.all_to_all(send_index, ('span', 'group'), split_axis=0, concat_axis=0...  11.5 us
    all_to_all x1, waiting for transfers between devices, per_device(): lax.all_to_all(reply, ('span', 'group'), split_axis=0, concat_axis=0, til...  10.8 us
  transfers between devices with their start and end apart: 15, of which 6 were waited for; matrix products, arithmetic and copies ran while one was open for 33% of the time, Pallas kernels for 0%

profile of v1, /device:TPU:1, one launch (start us, length us, event | category | flops | bytes accessed | tf_op | source)
XLA Modules:
  0.0 200.9 jit_solution(13995106509504392878)
XLA Ops:
  4.9 4.3 %scatter_custom_fusion = s32[2048]{0:T(1024)S(1)} fusion(s32[1024]{0:T(1024)S(1)} %bitcast.55, s32[1024]{0:T(1024)S(1)} %broadcast_select_fusion, s32[]{:T(128)} %constant.18.clone.1), kind=kCustom, calls=%fused_computation.81 | custom fusion | bytes 8196 | tf_op jit(solution)/shard_map/scatter | solution.py:83
  10.0 11.5 %all-to-all-start = ((s32[128,16,1]{1,2,0:T(1,128)}), s32[128,16,1]{1,2,0:T(1,128)S(1)}, u32[]{:S(2)}, u32[]{:S(2)}) async-start(s32[128,16,1]{1,2,0:T(1,128)} %bitcast.9), calls=%async_computation | async-start | bytes 131072 | tf_op jit(solution)/shard_map/all_to_all | solution.py:88
  23.7 2.2 %collective-permute-start.1 = (f32[1,1,8192]{2,1,0:T(1,128)S(1)}, f32[1,1,8192]{2,1,0:T(1,128)S(1)}, u32[]{:S(2)}, u32[]{:S(2)}) collective-permute-start(f32[1,1,8192]{2,1,0:T(1,128)S(1)} %get-tuple-element.28), channel_id=1, source_target_pairs={{0,8},{8,16},{16,24},{24,32},{32,40},{40,48},{48,56},{56,64},{64,7... | collective-permute-start | bytes 98312 | tf_op jit(solution)/shard_map/ppermute | solution.py:22
  25.9 2.2 %fusion.58 = (f32[1,16,8191]{2,1,0:T(8,128)S(1)}, f32[1,16,8191]{2,1,0:T(8,128)}) fusion(f32[1,16,8192]{2,1,0:T(8,128)} %param.11), kind=kLoop, calls=%fused_computation.100 | loop fusion | bytes 2096896 | tf_op jit(solution)/shard_map/slice | solution.py:35
  32.6 2.8 %gather_fusion = f32[1024,64]{1,0:T(8,128)S(1)} fusion(f32[2048,64]{1,0:T(8,128)S(1)} %reshape.278, s32[1024]{0:T(1024)S(1)} %get-tuple-element.34), kind=kCustom, calls=%fused_computation | custom fusion | bytes 528384 | tf_op jit(solution)/shard_map/gather | solution.py:69
  35.4 3.9 %scatter_custom_fusion.1 = f32[2048,64]{1,0:T(8,128)S(1)} fusion(s32[1024]{0:T(1024)S(1)} %bitcast.57, f32[1024,64]{1,0:T(8,128)S(1)} %gather_fusion, f32[]{:T(128)} %constant.20.clone.1, pred[1024]{0:T(1024)(128)(4,1)S(1)} %iota_compare_fusion.4), kind=kCustom, calls=%fused_computation.52 | custom fusion | flops 65536 | bytes 1050624 | tf_op jit(solution)/shard_map/scatter | solution.py:78
  39.4 1.5 reshape.396
  40.9 7.8 %copy.30 = bf16[128,4,4096]{0,2,1:T(8,128)(2,1)} copy(bf16[128,4,4096]{2,1,0:T(4,128)(2,1)} %param.16) | data formatting | bytes 8388608 | tf_op args[5]
  48.8 15.7 %copy.33 = bf16[128,4,64,64]{2,3,1,0:T(8,128)(2,1)} copy(bf16[128,4,64,64]{0,3,2,1:T(8,128)(2,1)} %bitcast.44) | data formatting | bytes 8388608 | tf_op jit(solution)/shard_map/reshape | solution.py:97
  64.5 11.6 %all-to-all-start.1 = ((f32[128,1,1024]{2,1,0:T(1,128)}), f32[128,1,1024]{2,1,0:T(1,128)S(1)}, u32[]{:S(2)}, u32[]{:S(2)}) async-start(f32[128,1,1024]{2,1,0:T(1,128)} %reshape.396), calls=%async_computation.1 | async-start | bytes 1048576 | tf_op jit(solution)/shard_map/all_to_all | solution.py:85
  76.7 7.6 %gather_fusion.1 = f32[2048,64]{1,0:T(8,128)} fusion(f32[128,64]{1,0:T(8,128)S(1)} %copy.28, s32[2048]{0:T(1024)S(1)} %broadcast_clamp_fusion), kind=kCustom, calls=%fused_computation.1 | custom fusion | bytes 1056768 | tf_op jit(solution)/shard_map/gather | solution.py:93
  84.3 1.5 fusion.6
  87.2 2.2 %collective-permute-start.3 = (f32[1,1,8192]{2,1,0:T(1,128)S(1)}, f32[1,1,8192]{2,1,0:T(1,128)S(1)}, u32[]{:S(2)}, u32[]{:S(2)}) collective-permute-start(f32[1,1,8192]{2,1,0:T(1,128)S(1)} %get-tuple-element.22), channel_id=1, source_target_pairs={{0,8},{8,16},{16,24},{24,32},{32,40},{40,48},{48,56},{56,64},{64,7... | collective-permute-start | bytes 98312 | tf_op jit(solution)/shard_map/ppermute | solution.py:22
  89.4 1.5 collective-permute-done.2
  91.0 2.0 %collective-permute-done.3 = f32[1,1,8192]{2,1,0:T(1,128)S(1)} collective-permute-done((f32[1,1,8192]{2,1,0:T(1,128)S(1)}, f32[1,1,8192]{2,1,0:T(1,128)S(1)}, u32[]{:S(2)}, u32[]{:S(2)}) %collective-permute-start.3) | collective-permute-done | bytes 32800 | tf_op jit(solution)/shard_map/ppermute | solution.py:22
  93.7 6.5 %collective-permute-start.4 = (f32[1,1,8192]{2,1,0:T(1,128)S(1)}, f32[1,1,8192]{2,1,0:T(1,128)S(1)}, u32[]{:S(2)}, u32[]{:S(2)}) collective-permute-start(f32[1,1,8192]{2,1,0:T(1,128)S(1)} %get-tuple-element.17), channel_id=1, source_target_pairs={{8,0},{16,8},{24,16},{32,24},{40,32},{48,40},{56,48},{64,56},{72,6... | collective-permute-start | bytes 98312 | tf_op jit(solution)/shard_map/ppermute | solution.py:25
  103.6 1.8 reduce.6
  106.6 1.9 fusion.1
  108.5 11.6 %scatter_fusion = f32[128,64]{1,0:T(8,128)S(1)} fusion(f32[128,64]{1,0:T(8,128)S(1)} %copy.28, s32[2048]{0:T(1024)S(1)} %reshape.347, f32[2048,64]{1,0:T(8,128)S(1)} %fusion.1), kind=kCustom, calls=%fused_computation.8 | custom fusion | flops 131072 | bytes 1581056 | tf_op jit(solution)/shard_map/scatter-add | solution.py:94
  120.1 3.2 %collective-permute-start.8 = (bf16[128,64]{1,0:T(8,128)(2,1)S(1)}, bf16[128,64]{1,0:T(8,128)(2,1)S(1)}, u32[]{:S(2)}, u32[]{:S(2)}) collective-permute-start(bf16[128,64]{1,0:T(8,128)(2,1)S(1)} %convert_element_type.15), channel_id=1, source_target_pairs={{0,1},{1,2},{2,3},{3,4},{4,5},{5,6},{6,7},{7,8},{8,9},{9,10},{10,1... | collective-permute-start | bytes 49160 | tf_op jit(solution)/shard_map/ppermute | solution.py:22
  123.4 9.0 %collective-permute-start.9 = (bf16[128,64]{1,0:T(8,128)(2,1)S(1)}, bf16[128,64]{1,0:T(8,128)(2,1)S(1)}, u32[]{:S(2)}, u32[]{:S(2)}) collective-permute-start(bf16[128,64]{1,0:T(8,128)(2,1)S(1)} %convert_element_type.15), channel_id=1, source_target_pairs={{1,0},{2,1},{3,2},{4,3},{5,4},{6,5},{7,6},{8,7},{9,8},{10,9},{11,1... | collective-permute-start | bytes 49160 | tf_op jit(solution)/shard_map/ppermute | solution.py:25
  134.7 4.8 %fusion.35 = f32[128,1,64,1]{2,1,3,0:T(1,128)S(1)} fusion(bf16[128,4,64,64]{2,3,1,0:T(8,128)(2,1)} %copy.33, bf16[128,4,64,1]{2,1,0,3:T(4,128)(2,1)S(1)} %bitcast.49), kind=kOutput, calls=%fused_computation.61 | convolution fusion | flops 4194304 | bytes 4292608 | tf_op jit(solution)/shard_map/bkij,bkj->bi/dot_general | solution.py:103
  139.5 1.9 collective-permute-start.10
  141.5 6.3 %collective-permute-start.11 = (bf16[128,64]{1,0:T(8,128)(2,1)S(1)}, bf16[128,64]{1,0:T(8,128)(2,1)S(1)}, u32[]{:S(2)}, u32[]{:S(2)}) collective-permute-start(bf16[128,64]{1,0:T(8,128)(2,1)S(1)} %get-tuple-element.8), channel_id=1, source_target_pairs={{1,0},{2,1},{3,2},{4,3},{5,4},{6,5},{7,6},{8,7},{9,8},{10,9},{11,1... | collective-permute-start | bytes 49160 | tf_op jit(solution)/shard_map/ppermute | solution.py:25
  147.9 3.2 %collective-permute-start.7 = (f32[1,1,8192]{2,1,0:T(1,128)S(1)}, f32[1,1,8192]{2,1,0:T(1,128)S(1)}, u32[]{:S(2)}, u32[]{:S(2)}) collective-permute-start(f32[1,1,8192]{2,1,0:T(1,128)S(1)} %get-tuple-element.10), channel_id=1, source_target_pairs={{0,8},{8,16},{16,24},{24,32},{32,40},{40,48},{48,56},{56,64},{64,7... | collective-permute-start | bytes 98312 | tf_op jit(solution)/shard_map/ppermute | solution.py:22
  152.5 4.8 %fusion.33 = f32[128,1,64,1]{2,1,3,0:T(1,128)S(1)} fusion(bf16[128,4,64,64]{2,3,1,0:T(8,128)(2,1)} %copy.33, bf16[128,4,64,1]{2,1,0,3:T(4,128)(2,1)S(1)} %bitcast.48), kind=kOutput, calls=%fused_computation.59 | convolution fusion | flops 4194304 | bytes 4292608 | tf_op jit(solution)/shard_map/bkij,bkj->bi/dot_general | solution.py:103
  157.3 5.5 %gather_fusion.4 = f32[2048,64]{1,0:T(8,128)S(1)} fusion(f32[128,64]{1,0:T(8,128)S(1)} %add.137, s32[2048]{0:T(1024)S(1)} %broadcast_clamp_fusion), kind=kCustom, calls=%fused_computation.4 | custom fusion | bytes 1056768 | tf_op jit(solution)/shard_map/gather | solution.py:106
  164.2 9.0 %all-to-all-start.2 = ((f32[128,1,1024]{2,1,0:T(1,128)}), f32[128,1,1024]{2,1,0:T(1,128)}, u32[]{:S(2)}, u32[]{:S(2)}) async-start(f32[128,1,1024]{2,1,0:T(1,128)} %reshape.398), calls=%async_computation.2 | async-start | bytes 1048576 | tf_op jit(solution)/shard_map/all_to_all | solution.py:107
  173.3 1.6 fusion.21
  176.0 10.8 %all-to-all-done.2 = f32[128,1,1024]{2,1,0:T(1,128)} async-done(((f32[128,1,1024]{2,1,0:T(1,128)}), f32[128,1,1024]{2,1,0:T(1,128)}, u32[]{:S(2)}, u32[]{:S(2)}) %all-to-all-start.2) | async-done | bytes 524320 | tf_op jit(solution)/shard_map/all_to_all | solution.py:107
  186.9 2.8 %reduce.7 = f32[128,1024]{1,0:T(8,128)S(1)} reduce(f32[128,1,1024]{2,1,0:T(1,128)} %all-to-all-done.2, f32[]{:T(128)} %broadcast.125), dimensions={1}, to_apply=%all_to_all.28.reduce_sub_computation | reduce | bytes 1048580 | tf_op jit(solution)/shard_map/all_to_all | solution.py:107
  190.0 9.7 %scatter_custom_fusion.3 = f32[2048,64]{1,0:T(8,128)S(1)} fusion(f32[2048,64]{1,0:T(8,128)S(1)} %reshape.276, s32[1024]{0:T(1024)S(1)} %get-tuple-element.35, f32[1024,64]{1,0:T(8,128)S(1)} %gather_fusion, f32[]{:T(128)} %constant.15.clone.1, f32[]{:T(128)} %constant.20.clone.1, pred[1024]{0:T(1024)(128)(4,1)S(1)} %iota_compare_fusion.4, ...), kind=kCustom, calls=%fused_computation.48 | custom fusion | flops 262144 | bytes 2102280 | tf_op jit(solution)/shard_map/scatter-add | solution.py:110
  (77 shorter events, 25.7 us)
Async XLA Ops:
  0.6 40.2 %copy-start.3 = (f32[128,64]{0,1:T(8,128)S(1)}, f32[128,64]{0,1:T(8,128)}, u32[]{:S(2)}) copy-start(f32[128,64]{0,1:T(8,128)} %param.15) | copy-start | bytes 98308
  10.0 54.5 %all-to-all-start = ((s32[128,16,1]{1,2,0:T(1,128)}), s32[128,16,1]{1,2,0:T(1,128)S(1)}, u32[]{:S(2)}, u32[]{:S(2)}) async-start(s32[128,16,1]{1,2,0:T(1,128)} %bitcast.9), calls=%async_computation | async-start | bytes 131072 | tf_op jit(solution)/shard_map/all_to_all | solution.py:88
  22.5 61.7 %collective-permute-start = (f32[1,1,8192]{2,1,0:T(1,128)S(1)}, f32[1,1,8192]{2,1,0:T(1,128)S(1)}, u32[]{:S(2)}, u32[]{:S(2)}) collective-permute-start(f32[1,1,8192]{2,1,0:T(1,128)S(1)} %get-tuple-element.29), channel_id=1, source_target_pairs={{8,0},{16,8},{24,16},{32,24},{40,32},{48,40},{56,48},{64,56},{72,6... | collective-permute-start | bytes 98312 | tf_op jit(solution)/shard_map/ppermute | solution.py:25
  23.7 60.6 %collective-permute-start.1 = (f32[1,1,8192]{2,1,0:T(1,128)S(1)}, f32[1,1,8192]{2,1,0:T(1,128)S(1)}, u32[]{:S(2)}, u32[]{:S(2)}) collective-permute-start(f32[1,1,8192]{2,1,0:T(1,128)S(1)} %get-tuple-element.28), channel_id=1, source_target_pairs={{0,8},{8,16},{16,24},{24,32},{32,40},{40,48},{48,56},{56,64},{64,7... | collective-permute-start | bytes 98312 | tf_op jit(solution)/shard_map/ppermute | solution.py:22
  64.5 19.8 %copy-start = (f32[1,16,8192]{2,1,0:T(8,128)S(1)}, f32[1,16,8192]{2,1,0:T(8,128)}, u32[]{:S(2)}) copy-start(f32[1,16,8192]{2,1,0:T(8,128)} %param.11) | copy-start | bytes 1572868
  64.5 19.8 %copy-start.1 = (f32[1,16,8192]{2,1,0:T(8,128)S(1)}, f32[1,16,8192]{2,1,0:T(8,128)}, u32[]{:S(2)}) copy-start(f32[1,16,8192]{2,1,0:T(8,128)} %param.13) | copy-start | bytes 1572868
  64.5 19.8 %copy-start.2 = (f32[1,16,8192]{2,1,0:T(8,128)S(1)}, f32[1,16,8192]{2,1,0:T(8,128)}, u32[]{:S(2)}) copy-start(f32[1,16,8192]{2,1,0:T(8,128)} %param.12) | copy-start | bytes 1572868
  64.5 38.6 %all-to-all-start.1 = ((f32[128,1,1024]{2,1,0:T(1,128)}), f32[128,1,1024]{2,1,0:T(1,128)S(1)}, u32[]{:S(2)}, u32[]{:S(2)}) async-start(f32[128,1,1024]{2,1,0:T(1,128)} %reshape.396), calls=%async_computation.1 | async-start | bytes 1048576 | tf_op jit(solution)/shard_map/all_to_all | solution.py:85
  86.0 4.9 %collective-permute-start.2 = (f32[1,1,8192]{2,1,0:T(1,128)S(1)}, f32[1,1,8192]{2,1,0:T(1,128)S(1)}, u32[]{:S(2)}, u32[]{:S(2)}) collective-permute-start(f32[1,1,8192]{2,1,0:T(1,128)S(1)} %get-tuple-element.23), channel_id=1, source_target_pairs={{8,0},{16,8},{24,16},{32,24},{40,32},{48,40},{56,48},{64,56},{72,6... | collective-permute-start | bytes 98312 | tf_op jit(solution)/shard_map/ppermute | solution.py:25
  87.2 5.8 %collective-permute-start.3 = (f32[1,1,8192]{2,1,0:T(1,128)S(1)}, f32[1,1,8192]{2,1,0:T(1,128)S(1)}, u32[]{:S(2)}, u32[]{:S(2)}) collective-permute-start(f32[1,1,8192]{2,1,0:T(1,128)S(1)} %get-tuple-element.22), channel_id=1, source_target_pairs={{0,8},{8,16},{16,24},{24,32},{32,40},{40,48},{48,56},{56,64},{64,7... | collective-permute-start | bytes 98312 | tf_op jit(solution)/shard_map/ppermute | solution.py:22
  93.7 7.4 %collective-permute-start.4 = (f32[1,1,8192]{2,1,0:T(1,128)S(1)}, f32[1,1,8192]{2,1,0:T(1,128)S(1)}, u32[]{:S(2)}, u32[]{:S(2)}) collective-permute-start(f32[1,1,8192]{2,1,0:T(1,128)S(1)} %get-tuple-element.17), channel_id=1, source_target_pairs={{8,0},{16,8},{24,16},{32,24},{40,32},{48,40},{56,48},{64,56},{72,6... | collective-permute-start | bytes 98312 | tf_op jit(solution)/shard_map/ppermute | solution.py:25
  100.2 1.2 collective-permute-start.5
  120.1 12.3 %collective-permute-start.8 = (bf16[128,64]{1,0:T(8,128)(2,1)S(1)}, bf16[128,64]{1,0:T(8,128)(2,1)S(1)}, u32[]{:S(2)}, u32[]{:S(2)}) collective-permute-start(bf16[128,64]{1,0:T(8,128)(2,1)S(1)} %convert_element_type.15), channel_id=1, source_target_pairs={{0,1},{1,2},{2,3},{3,4},{4,5},{5,6},{6,7},{7,8},{8,9},{9,10},{10,1... | collective-permute-start | bytes 49160 | tf_op jit(solution)/shard_map/ppermute | solution.py:22
  123.4 10.0 %collective-permute-start.9 = (bf16[128,64]{1,0:T(8,128)(2,1)S(1)}, bf16[128,64]{1,0:T(8,128)(2,1)S(1)}, u32[]{:S(2)}, u32[]{:S(2)}) collective-permute-start(bf16[128,64]{1,0:T(8,128)(2,1)S(1)} %convert_element_type.15), channel_id=1, source_target_pairs={{1,0},{2,1},{3,2},{4,3},{5,4},{6,5},{7,6},{8,7},{9,8},{10,9},{11,1... | collective-permute-start | bytes 49160 | tf_op jit(solution)/shard_map/ppermute | solution.py:25
  139.5 11.6 %collective-permute-start.10 = (bf16[128,64]{1,0:T(8,128)(2,1)S(1)}, bf16[128,64]{1,0:T(8,128)(2,1)S(1)}, u32[]{:S(2)}, u32[]{:S(2)}) collective-permute-start(bf16[128,64]{1,0:T(8,128)(2,1)S(1)} %get-tuple-element.8), channel_id=1, source_target_pairs={{0,1},{1,2},{2,3},{3,4},{4,5},{5,6},{6,7},{7,8},{8,9},{9,10},{10,1... | collective-permute-start | bytes 49160 | tf_op jit(solution)/shard_map/ppermute | solution.py:22
  141.5 9.7 %collective-permute-start.11 = (bf16[128,64]{1,0:T(8,128)(2,1)S(1)}, bf16[128,64]{1,0:T(8,128)(2,1)S(1)}, u32[]{:S(2)}, u32[]{:S(2)}) collective-permute-start(bf16[128,64]{1,0:T(8,128)(2,1)S(1)} %get-tuple-element.8), channel_id=1, source_target_pairs={{1,0},{2,1},{3,2},{4,3},{5,4},{6,5},{7,6},{8,7},{9,8},{10,9},{11,1... | collective-permute-start | bytes 49160 | tf_op jit(solution)/shard_map/ppermute | solution.py:25
  147.9 25.4 %collective-permute-start.6 = (f32[1,1,8192]{2,1,0:T(1,128)S(1)}, f32[1,1,8192]{2,1,0:T(1,128)S(1)}, u32[]{:S(2)}, u32[]{:S(2)}) collective-permute-start(f32[1,1,8192]{2,1,0:T(1,128)S(1)} %get-tuple-element.11), channel_id=1, source_target_pairs={{8,0},{16,8},{24,16},{32,24},{40,32},{48,40},{56,48},{64,56},{72,6... | collective-permute-start | bytes 98312 | tf_op jit(solution)/shard_map/ppermute | solution.py:25
  147.9 25.4 %collective-permute-start.7 = (f32[1,1,8192]{2,1,0:T(1,128)S(1)}, f32[1,1,8192]{2,1,0:T(1,128)S(1)}, u32[]{:S(2)}, u32[]{:S(2)}) collective-permute-start(f32[1,1,8192]{2,1,0:T(1,128)S(1)} %get-tuple-element.10), channel_id=1, source_target_pairs={{0,8},{8,16},{16,24},{24,32},{32,40},{40,48},{48,56},{56,64},{64,7... | collective-permute-start | bytes 98312 | tf_op jit(solution)/shard_map/ppermute | solution.py:22
  164.2 22.6 %all-to-all-start.2 = ((f32[128,1,1024]{2,1,0:T(1,128)}), f32[128,1,1024]{2,1,0:T(1,128)}, u32[]{:S(2)}, u32[]{:S(2)}) async-start(f32[128,1,1024]{2,1,0:T(1,128)} %reshape.398), calls=%async_computation.2 | async-start | bytes 1048576 | tf_op jit(solution)/shard_map/all_to_all | solution.py:107

commit v2 on v1

v2 whole, which is shorter than its diff:
```python
import functools

import jax
import jax.numpy as jnp
from jax import lax
from jax.experimental import pallas as pl
from jax.experimental.pallas import tpu as pltpu
from jax.sharding import PartitionSpec as P

STEPS = 4
SSTEPS = 2
NODES = 64
CAP = 16
LANES = 128
UPTAKE = 0.3
RELEASE = 0.5
MESH = pl.DeviceIdType.MESH
F32 = jnp.float32
BF16 = jnp.bfloat16
I32 = jnp.int32


def iota(shape, dim):
    return lax.broadcasted_iota(I32, shape, dim)


def onehot(mask):
    return jnp.where(mask, F32(1.0), F32(0.0)).astype(BF16)


def mm(a, b):
    return jnp.dot(a, b, preferred_element_type=F32)


def mm_nt(a, b):
    return lax.dot_general(a, b, (((1,), (1,)), ((), ())), preferred_element_type=F32)


def split(x):
    hi = x.astype(BF16)
    lo = (x - hi.astype(F32)).astype(BF16)
    return hi, lo


def kernel(
    nspan,
    ngroup,
    air_h,
    vel_h,
    kap_h,
    width_s,
    sub_h,
    c_h,
    nbr_h,
    count_s,
    seg_h,
    own_h,
    blk_h,
    air_o,
    sub_o,
    air_v,
    vel_v,
    kap_v,
    sub_v,
    c_v,
    nbr_v,
    seg_v,
    own_v,
    blk_v,
    field,
    bank,
    pick,
    send,
    recv,
    back,
    got,
    idx_out,
    idx_in,
    t_v,
    tt_v,
    pt_v,
    st_v,
    near_map,
    near_v,
    z_v,
    beside,
    edge_lo,
    edge_hi,
    halo_w,
    halo_e,
    in_sem,
    send_sem,
    recv_sem,
    edge_send,
    edge_recv,
    side_send,
    side_recv,
):
    ndev = nspan * ngroup
    span = lax.axis_index("span")
    group = lax.axis_index("group")
    me = span * ngroup + group

    def where_is(d):
        return (d // ngroup, d % ngroup)

    loads = []
    for k, (src, dst) in enumerate(
        (
            (own_h, own_v),
            (seg_h, seg_v),
            (blk_h, blk_v),
            (air_h, air_v),
            (nbr_h, nbr_v),
            (sub_h, sub_v),
            (vel_h, vel_v),
            (kap_h, kap_v),
            (c_h, c_v),
        )
    ):
        copy = pltpu.make_async_copy(src, dst, in_sem.at[k])
        copy.start()
        loads.append(copy)

    barrier = pltpu.get_barrier_semaphore()

    @pl.loop(1, ndev)
    def _(i):
        pl.semaphore_signal(
            barrier, inc=1, device_id=where_is((me + i) % ndev), device_id_type=MESH
        )

    count = count_s[0]
    width = width_s[0]
    lane = iota((1, LANES), 1)

    for k in range(3):
        loads[k].wait()
    own8 = own_v[...]
    seg8 = seg_v[...]
    blk8 = blk_v[...]
    active8 = (iota((8, LANES), 0) * LANES + iota((8, LANES), 1)) < count
    sub128 = iota((LANES, LANES), 0)
    hits = [own8[c : c + 1, :] == sub128 for c in range(8)]
    upper = onehot(iota((LANES, 2 * LANES), 0) < iota((LANES, 2 * LANES), 1))
    ahead = mm(jnp.concatenate([onehot(h) for h in hits], axis=0), upper)
    carry = jnp.zeros((LANES, LANES), F32)
    ranks = []
    for c in range(8):
        part = ahead[c * LANES : (c + 1) * LANES]
        ranks.append(
            jnp.sum(jnp.where(hits[c], part[:, :LANES] + carry, F32(0.0)), axis=0, keepdims=True)
        )
        carry = carry + part[:, LANES:]
    rank8 = jnp.concatenate(ranks, axis=0)
    place8 = jnp.where(active8, own8 * CAP + rank8.astype(I32), -1)
    line8 = seg8 // LANES
    key8 = (line8 // 8) * 512 + ((seg8 % LANES) // 2) * 8 + line8 % 8
    half8 = seg8 % 2
    shift8 = jnp.where(active8, rank8.astype(I32) + (me % 8) * CAP, -1)
    table = jnp.concatenate(
        [
            place8.astype(F32),
            key8.astype(F32),
            half8.astype(F32),
            shift8.astype(F32),
            (blk8 + 1).astype(F32),
            active8.astype(F32),
            jnp.zeros((LANES - 48, LANES), F32),
        ],
        axis=0,
    )
    columns = table.T.astype(I32)

    def column(a, c):
        return columns[:, a * 8 + c : a * 8 + c + 1]

    slots = jnp.concatenate(
        [
            jnp.where(column(3, c) == lane, column(4, c).astype(F32), F32(0.0)).astype(BF16)
            for c in range(8)
        ],
        axis=0,
    )
    owners = jnp.concatenate([onehot(h) for h in hits], axis=1)
    idx_out[...] = mm(owners, slots)

    loads[3].wait()
    for line in range(2):
        for j in range(64):
            k = (line * 64 + j) * 8
            a = air_v[line * 8 : line * 8 + 8, j * LANES : (j + 1) * LANES]
            hi = a.astype(BF16).astype(F32)
            lo = a - hi
            z_v[k : k + 8, :LANES] = jnp.where(lane < 64, hi, pltpu.roll(lo, 64, 1))
            z_v[k : k + 8, LANES:] = jnp.where(lane < 64, pltpu.roll(hi, 64, 1), lo)
    bank[...] = z_v[...].astype(BF16)
    key_lane = iota((LANES, 8 * LANES), 1)
    for c in range(8):
        rows = mm(onehot(column(1, c) == key_lane), bank[...])
        pick[c * LANES : (c + 1) * LANES, :] = jnp.where(
            column(2, c) == 0, rows[:, :LANES], rows[:, LANES:]
        ).astype(BF16)

    @pl.loop(0, 8)
    def _(q):
        slot = iota((256, LANES), 0) + q * 256
        sel = jnp.concatenate([onehot(place8[c : c + 1, :] == slot) for c in range(8)], axis=1)
        send[pl.ds(q * 16, 16)] = mm(sel, pick[...]).astype(BF16).reshape(16, CAP, LANES)

    edge_lo[0] = air_v[0:1, :]
    edge_hi[0] = air_v[15:16, :]
    field[:, LANES : LANES + 8192] = air_v[...]

    def pad_ends():
        field[:, :LANES] = jnp.broadcast_to(field[:, LANES : LANES + 1], (16, LANES))
        field[:, LANES + 8192 :] = jnp.broadcast_to(
            field[:, LANES + 8191 : LANES + 8192], (16, LANES)
        )

    pad_ends()

    pl.semaphore_wait(barrier, ndev - 1)

    def edges(step):
        east = ((span + 1) % nspan, group)
        west = ((span + nspan - 1) % nspan, group)
        return (
            pltpu.make_async_remote_copy(
                edge_hi.at[step], halo_w.at[step], edge_send.at[step, 0], edge_recv.at[step, 0],
                device_id=east, device_id_type=MESH,
            ),
            pltpu.make_async_remote_copy(
                edge_lo.at[step], halo_e.at[step], edge_send.at[step, 1], edge_recv.at[step, 1],
                device_id=west, device_id_type=MESH,
            ),
        )

    for e in edges(0):
        e.start()

    def scatter_all(src, dst, k):
        @pl.loop(1, ndev)
        def _(i):
            d = (me + i) % ndev
            pltpu.make_async_remote_copy(
                src.at[d], dst.at[me], send_sem.at[k], recv_sem.at[k],
                device_id=where_is(d), device_id_type=MESH,
            ).start()

    def whole(src, dst, k):
        return pltpu.make_async_remote_copy(
            src.at[pl.ds(0, ndev - 1)], dst.at[pl.ds(0, ndev - 1)], send_sem.at[k], recv_sem.at[k],
            device_id=where_is((me + 1) % ndev), device_id_type=MESH,
        )

    scatter_all(send, recv, 0)
    scatter_all(idx_out, idx_in, 1)
    recv[me] = send[me]
    idx_in[pl.ds(me, 1), :] = idx_out[pl.ds(me, 1), :]

    for c in range(8):
        slot_lane = iota((LANES, 2048), 1)
        pt_v[c * LANES : (c + 1) * LANES, :] = onehot(column(0, c) == slot_lane)

    @pl.loop(0, 8)
    def _(q):
        at = iota((LANES, LANES), 0) + q * LANES
        st_v[pl.ds(q * LANES, LANES), :] = jnp.concatenate(
            [onehot(key8[c : c + 1, :] == at) for c in range(8)], axis=1
        )

    loads[4].wait()
    nbr = (nbr_v[...] - (me - 1) * LANES).astype(F32)
    nbr8 = jnp.concatenate([nbr, nbr], axis=0)

    @pl.loop(0, 8)
    def _(q):
        tiled = jnp.concatenate([nbr8] * 16, axis=0)
        own_lane = (iota((LANES, LANES), 0) // 8 + q * 16) == iota((LANES, LANES), 1)
        link = jnp.sum(jnp.where(own_lane, tiled, F32(0.0)), axis=1, keepdims=True).astype(I32)
        near_map[pl.ds(q * LANES, LANES), :] = onehot(link == iota((LANES, 3 * LANES), 1))

    loads[6].wait()
    loads[7].wait()

    def advance(step):
        for e in edges(step):
            e.wait()
        wide = 1024
        row = iota((16, wide), 0)
        fresh = []
        for j in range(8192 // wide):
            ext = field[:, j * wide : j * wide + wide + 2 * LANES]
            t = ext[:, LANES : LANES + wide]
            north = pltpu.roll(ext, wide + 2 * LANES - 1, 1)[:, LANES : LANES + wide]
            south = pltpu.roll(ext, 1, 1)[:, LANES : LANES + wide]
            cut = slice(j * wide, (j + 1) * wide)
            east = jnp.where(row == 15, halo_e[step, :, cut], pltpu.roll(t, 15, 0))
            west = jnp.where(row == 0, halo_w[step, :, cut], pltpu.roll(t, 1, 0))
            new = (
                t
                + kap_v[:, cut] * ((east + west) + (north + south) - 4.0 * t)
                - (0.5 * vel_v[:, cut]) * (east - west)
            )
            new = jnp.where(iota((16, wide), 1) + j * wide < width, new, t)
            air_v[:, cut] = new
        field[:, LANES : LANES + 8192] = air_v[...]
        if step + 1 < STEPS:
            pad_ends()
            edge_lo[step + 1] = air_v[0:1, :]
            edge_hi[step + 1] = air_v[15:16, :]
            for e in edges(step + 1):
                e.start()

    advance(0)

    loads[5].wait()
    sub = jnp.concatenate([sub_v[...], sub_v[...]], axis=0).T
    both = whole(idx_out, idx_in, 1)
    both.wait_send()
    both.wait_recv()
    for q in range(16):
        at = jnp.sum(idx_in[q * 8 : q * 8 + 8, :], axis=0, keepdims=True).astype(I32)
        t_q = jnp.where(at == iota((LANES, LANES), 0) + 1, F32(1.0), F32(0.0))
        t_v[:, q * LANES : (q + 1) * LANES] = t_q.astype(BF16)
        tt_v[q * LANES : (q + 1) * LANES, :] = t_q.T.astype(BF16)
    hits_b = mm(t_v[...], jnp.ones((2048, LANES), BF16))
    both = whole(send, recv, 0)
    both.wait_send()
    both.wait_recv()
    total = mm(t_v[...], recv[...].reshape(2048, LANES))
    total = total + pltpu.roll(total, 64, 1)
    sub = sub + UPTAKE * (total - hits_b * sub)

    def sides(step):
        nxt = where_is((me + 1) % ndev)
        prev = where_is((me + ndev - 1) % ndev)
        return (
            pltpu.make_async_remote_copy(
                beside.at[step, 1], beside.at[step, 0], side_send.at[step, 0], side_recv.at[step, 0],
                device_id=nxt, device_id_type=MESH,
            ),
            pltpu.make_async_remote_copy(
                beside.at[step, 1], beside.at[step, 2], side_send.at[step, 1], side_recv.at[step, 1],
                device_id=prev, device_id_type=MESH,
            ),
        )

    lane2 = iota((LANES, LANES), 1)
    row2 = iota((LANES, LANES), 0)
    gather_i = onehot((lane2 % 64) // 2 == row2 // 4)
    gather_i = jnp.concatenate([gather_i, gather_i], axis=0)
    per_block = onehot(iota((LANES, 8 * LANES), 1) // 8 == iota((LANES, 8 * LANES), 0))
    half_lane = (iota((8 * LANES, LANES), 0) % 8) // 4 == iota((8 * LANES, LANES), 1) // 64
    odd_lane = (iota((8 * LANES, LANES), 0) % 8) // 4 == iota((8 * LANES, LANES), 1) % 2
    same = iota((8, LANES), 0) % 4 == iota((8, LANES), 1) % 4

    for step in range(SSTEPS):
        beside[step, 1] = sub.astype(BF16)
        for s in sides(step):
            s.start()
        advance(step + 1)
        if step == 0:
            loads[8].wait()
        for s in sides(step):
            s.wait()
        near = mm(near_map[...], beside[step].reshape(3 * LANES, LANES))
        near_v[...] = jnp.where(half_lane, near, F32(0.0)).astype(BF16)

        @pl.loop(0, 64, unroll=8)
        def _(p):
            res = mm_nt(near_v[pl.ds(p * 16, 16), :], c_v[pl.ds(p * 256, 256), :])
            z_v[pl.ds(p * 16, 8), :LANES] = jnp.where(same, res[:8, :LANES], F32(0.0))
            z_v[pl.ds(p * 16 + 8, 8), :LANES] = jnp.where(same, res[8:, LANES:], F32(0.0))

        hi, lo = split(z_v[:, :LANES])
        w = mm(jnp.concatenate([hi, lo], axis=1), gather_i)
        hi, lo = split(jnp.where(odd_lane, w, F32(0.0)))
        added = mm(per_block, jnp.concatenate([hi, lo], axis=1))
        sub = sub + (added[:, :LANES] + added[:, LANES:])

    hi = sub.astype(BF16).astype(F32)
    pair = jnp.where(lane2 < 64, hi, sub - hi).astype(BF16)
    back[...] = mm(tt_v[...], pair).astype(BF16).reshape(ndev, CAP, LANES)
    scatter_all(back, got, 2)
    got[me] = back[me]
    sub_o[...] = sub.T[:64, :]
    advance(3)
    both = whole(back, got, 2)
    both.wait_send()
    both.wait_recv()

    for c in range(8):
        rows = slice(c * LANES, (c + 1) * LANES)
        surf = mm(pt_v[rows, :], got[...].reshape(2048, LANES))
        gap = surf - pick[rows, :].astype(F32)
        gap = RELEASE * (gap + pltpu.roll(gap, 64, 1))
        keep = jnp.logical_and(column(5, c) == 1, column(2, c) == lane2 // 64)
        hi, lo = split(jnp.where(keep, gap, F32(0.0)))
        bank[rows, :LANES] = hi
        bank[rows, LANES:] = lo
    z_v[...] = mm(st_v[...], bank[...])
    for line in range(2):
        for j in range(64):
            k = (line * 64 + j) * 8
            cut = slice(j * LANES, (j + 1) * LANES)
            air_o[line * 8 : line * 8 + 8, cut] = air_v[line * 8 : line * 8 + 8, cut] + (
                z_v[k : k + 8, :LANES] + z_v[k : k + 8, LANES:]
            )


def per_device(
    nspan,
    ngroup,
    air_temp,
    air_vel,
    air_kappa,
    group_width,
    sub_temp,
    sub_coupling,
    neighbors,
    iface_count,
    iface_seg,
    iface_owner,
    iface_block,
):
    cells, section = air_temp.shape[1:]
    blocks, links, _ = sub_coupling.shape
    coupling = (
        sub_coupling.reshape(blocks, links, 32, LANES)
        .transpose(0, 2, 1, 3)
        .reshape(blocks * links * 32, LANES)
    )
    ndev = nspan * ngroup
    vmem = pltpu.VMEM
    dma = pltpu.SemaphoreType.DMA
    any_space = pl.BlockSpec(memory_space=pl.ANY)
    smem = pl.BlockSpec(memory_space=pltpu.SMEM)
    in_vmem = pl.BlockSpec(memory_space=pltpu.VMEM)
    air, sub = pl.pallas_call(
        functools.partial(kernel, nspan, ngroup),
        out_shape=(
            jax.ShapeDtypeStruct((cells, section), F32),
            jax.ShapeDtypeStruct((NODES, blocks), F32),
        ),
        in_specs=[any_space] * 3 + [smem] + [any_space] * 3 + [smem] + [any_space] * 3,
        out_specs=(in_vmem, in_vmem),
        scratch_shapes=[
            vmem((cells, section), F32),
            vmem((cells, section), F32),
            vmem((cells, section), F32),
            vmem((NODES, blocks), F32),
            vmem(coupling.shape, BF16),
            vmem((links, blocks), I32),
            vmem((8, LANES), I32),
            vmem((8, LANES), I32),
            vmem((8, LANES), I32),
            vmem((cells, section + 2 * LANES), F32),
            vmem((8 * LANES, 2 * LANES), BF16),
            vmem((8 * LANES, LANES), BF16),
            vmem((ndev, CAP, LANES), BF16),
            vmem((ndev, CAP, LANES), BF16),
            vmem((ndev, CAP, LANES), BF16),
            vmem((ndev, CAP, LANES), BF16),
            vmem((ndev, LANES), F32),
            vmem((ndev, LANES), F32),
            vmem((LANES, ndev * CAP), BF16),
            vmem((ndev * CAP, LANES), BF16),
            vmem((8 * LANES, ndev * CAP), BF16),
            vmem((8 * LANES, 8 * LANES), BF16),
            vmem((8 * LANES, 3 * LANES), BF16),
            vmem((8 * LANES, LANES), BF16),
            vmem((8 * LANES, 2 * LANES), F32),
            vmem((SSTEPS, 3, LANES, LANES), BF16),
            vmem((STEPS, 1, section), F32),
            vmem((STEPS, 1, section), F32),
            vmem((STEPS, 1, section), F32),
            vmem((STEPS, 1, section), F32),
            dma((9,)),
            dma((3,)),
            dma((3,)),
            dma((STEPS, 2)),
            dma((STEPS, 2)),
            dma((SSTEPS, 2)),
            dma((SSTEPS, 2)),
        ],
        compiler_params=pltpu.CompilerParams(
            collective_id=0, has_side_effects=True, vmem_limit_bytes=56 << 20
        ),
    )(
        air_temp.reshape(cells, section),
        air_vel.reshape(cells, section),
        air_kappa.reshape(cells, section),
        group_width,
        sub_temp.T,
        coupling,
        neighbors.T,
        iface_count,
        iface_seg.reshape(8, LANES),
        iface_owner.reshape(8, LANES),
        iface_block.reshape(8, LANES),
    )
    return air.reshape(1, cells, section), sub.T


def solution(mesh):
    placed = (
        P("group", "span", None),
        P("group", "span", None),
        P("group", "span", None),
        P("group"),
        P(("span", "group"), None),
        P(("span", "group"), None, None),
        P(("span", "group"), None),
        P(("span", "group")),
        P(("span", "group")),
        P(("span", "group"), None),
        P(("span", "group")),
    )
    return jax.shard_map(
        functools.partial(per_device, mesh.shape["span"], mesh.shape["group"]),
        mesh=mesh,
        in_specs=placed,
        out_specs=(P("group", "span", None), P(("span", "group"), None)),
        check_vma=False,
    )
```

time: 202 us -> 56 us (0.28)
  starting transfers between devices: 69 us -> 0 us
  local copies, waits for them, and re-layouts: 63.1 us -> 3.24 us
  Pallas kernels: 0 us -> 50.6 us
  other arithmetic: 40.5 us -> 0 us
  waiting for transfers between devices: 16.5 us -> 0 us
  matrix products: 9.54 us -> 0 us
    pallas_call x0 -> x1, Pallas kernels: none -> 50.6 us  [per_device(): pl.pallas_call(functools.partial(kernel, nspan, ngroup), out_shape=(jax.S...]
    ppermute x12 -> x0, starting transfers between devices: 36.9 us -> none  [the longest x6 24.1 us: with_halo(): lax.ppermute(lax.slice_in_dim(block, 0, width, axis=dim), axis, backward)]
    all_to_all x3 -> x0, starting transfers between devices: 32.1 us -> none  [the longest x1 11.6 us: per_device(): lax.all_to_all(send_rows, ('span', 'group'), split_axis=0, concat_axis=0,...]
    scatter-add x2 -> x0, other arithmetic: 21.3 us -> none  [the longest x1 11.6 us: per_device(): substrate = sub_temp.at[target].add(gain)]
    reshape x4 -> x0, local copies, waits for them, and re-layouts: 18.7 us -> none  [the longest x1 15.7 us: per_device(): coupling = sub_coupling.reshape(blocks, links_count, NODES, NODES)]
    gather x5 -> x0, local copies, waits for them, and re-layouts: 18.5 us -> none  [the longest x1 7.57 us: per_device(): sub_temp[target]]
    all_to_all x3 -> x0, waiting for transfers between devices: 10.8 us -> none  [the longest x1 10.8 us: per_device(): lax.all_to_all(reply, ('span', 'group'), split_axis=0, concat_axis=0, til...]
    unnamed x15 -> x2, local copies, waits for them, and re-layouts: 13.1 us -> 3.24 us
  transfers between devices with their start and end apart: 15 -> 0, of which waited for: 6 -> 0; matrix products, arithmetic and copies ran while one was open for 33% -> 0% of each run, Pallas kernels for 0% -> 0%
where the time goes in v2:
time: 56 us; the launch traced here: 55.8 us
  Pallas kernels  50.6 us (90%)
  local copies, waits for them, and re-layouts  3.24 us (6%)
  between operations  1.93 us (3%)
    pallas_call x1, Pallas kernels, per_device(): pl.pallas_call(functools.partial(kernel, nspan, ngroup), out_shape=(jax.S...  50.6 us
    unnamed x2, local copies, waits for them, and re-layouts  3.24 us

profile of v2, /device:TPU:1, one launch (start us, length us, event | category | flops | bytes accessed | tf_op | source)
XLA Modules:
  0.0 55.8 jit_solution(10518814333619722953)
XLA Ops:
  1.9 50.6 %shard_map.122 = (f32[16,8192]{1,0:T(8,128)}, f32[64,128]{1,0:T(8,128)}) custom-call(f32[16,8192]{1,0:T(8,128)} %bitcast.16, f32[16,8192]{1,0:T(8,128)} %bitcast.17, f32[16,8192]{1,0:T(8,128)} %bitcast.18, s32[1]{0:T(128)S(6)} %copy.16.width_s, f32[64,128]{1,0:T(8,128)} %bitcast.20, bf16[16384,128]{1,0:T(8,128)(2,1)} %bitcast.15, s32[4,128]{1,0:T(4,128)} %bitcast.25, ...), custom_call_target="tpu_custom_call" | custom-call | tf_op jit(solution)/shard_map/pallas_call | solution.py:441
  52.5 1.9 %copy.18 = f32[1,16,8192]{2,1,0:T(8,128)} copy(f32[1,16,8192]{2,1,0:T(8,128)} %bitcast.19) | data formatting | bytes 1048576
  54.4 1.4 %copy.19 = f32[128,64]{0,1:T(8,128)} copy(f32[128,64]{0,1:T(8,128)} %bitcast.21) | data formatting | bytes 65536

commit v3 on v2

--- a/solution.py
+++ b/solution.py
@@ -75,6 +75,8 @@
     back,
     got,
     idx_out,
+    idx_row_in,
+    idx_mid,
     idx_in,
     t_v,
     tt_v,
@@ -95,6 +97,7 @@
     edge_recv,
     side_send,
     side_recv,
+    ready,
 ):
     ndev = nspan * ngroup
     span = lax.axis_index("span")
@@ -124,11 +127,10 @@
 
     barrier = pltpu.get_barrier_semaphore()
 
-    @pl.loop(1, ndev)
-    def _(i):
-        pl.semaphore_signal(
-            barrier, inc=1, device_id=where_is((me + i) % ndev), device_id_type=MESH
-        )
+    row_peers = [(span, (group + j) % ngroup) for j in range(ngroup)]
+    column_peers = [((span + i) % nspan, group) for i in range(nspan)]
+    for peer in row_peers[1:] + column_peers[1:]:
+        pl.semaphore_signal(barrier, inc=1, device_id=peer, device_id_type=MESH)
 
     count = count_s[0]
     width = width_s[0]
@@ -157,7 +159,7 @@
     line8 = seg8 // LANES
     key8 = (line8 // 8) * 512 + ((seg8 % LANES) // 2) * 8 + line8 % 8
     half8 = seg8 % 2
-    shift8 = jnp.where(active8, rank8.astype(I32) + (me % 8) * CAP, -1)
+    shift8 = jnp.where(active8, rank8.astype(I32) + group * CAP, -1)
     table = jnp.concatenate(
         [
             place8.astype(F32),
@@ -182,7 +184,8 @@
         ],
         axis=0,
     )
-    owners = jnp.concatenate([onehot(h) for h in hits], axis=1)
+    spot8 = (own8 % ngroup) * nspan + own8 // ngroup
+    owners = jnp.concatenate([onehot(spot8[c : c + 1, :] == sub128) for c in range(8)], axis=1)
     idx_out[...] = mm(owners, slots)
 
     loads[3].wait()
@@ -220,7 +223,22 @@
 
     pad_ends()
 
-    pl.semaphore_wait(barrier, ndev - 1)
+    pl.semaphore_wait(barrier, nspan + ngroup - 2)
+    for peer in row_peers[1:]:
+        pl.semaphore_signal(ready, inc=1, device_id=peer, device_id_type=MESH)
+
+    def idx_row(j):
+        g = (group + j) % ngroup
+        return pltpu.make_async_remote_copy(
+            idx_out.at[pl.ds(pl.multiple_of(g * nspan, nspan), nspan)],
+            idx_row_in.at[group],
+            send_sem.at[1], recv_sem.at[1],
+            device_id=(span, g), device_id_type=MESH,
+        )
+
+    for j in range(1, ngroup):
+        idx_row(j).start()
+    idx_row_in[group] = idx_out[pl.ds(pl.multiple_of(group * nspan, nspan), nspan), :]
 
     def edges(step):
         east = ((span + 1) % nspan, group)
@@ -240,13 +258,20 @@
         e.start()
 
     def scatter_all(src, dst, k):
-        @pl.loop(1, ndev)
+        def to(s, g):
+            pltpu.make_async_remote_copy(
+                src.at[s * ngroup + g], dst.at[me], send_sem.at[k], recv_sem.at[k],
+                device_id=(s, g), device_id_type=MESH,
+            ).start()
+
+        for s, g in row_peers[1:]:
+            to(s, g)
+
+        @pl.loop(1, nspan)
         def _(i):
-            d = (me + i) % ndev
-            pltpu.make_async_remote_copy(
-                src.at[d], dst.at[me], send_sem.at[k], recv_sem.at[k],
-                device_id=where_is(d), device_id_type=MESH,
-            ).start()
+            s = (span + i) % nspan
+            for _, g in row_peers:
+                to(s, g)
 
     def whole(src, dst, k):
         return pltpu.make_async_remote_copy(
@@ -254,10 +279,30 @@
             device_id=where_is((me + 1) % ndev), device_id_type=MESH,
         )
 
+    pl.semaphore_wait(ready, ngroup - 1)
     scatter_all(send, recv, 0)
-    scatter_all(idx_out, idx_in, 1)
     recv[me] = send[me]
-    idx_in[pl.ds(me, 1), :] = idx_out[pl.ds(me, 1), :]
+    both = pltpu.make_async_remote_copy(
+        idx_row_in.at[pl.ds(0, ngroup - 1)], idx_row_in.at[pl.ds(0, ngroup - 1)],
+        send_sem.at[1], recv_sem.at[1], device_id=row_peers[1], device_id_type=MESH,
+    )
+    both.wait_send()
+    both.wait_recv()
+    total = idx_row_in[0]
+    for g in range(1, ngroup):
+        total = total + idx_row_in[g]
+    idx_mid[:, 0, :] = total
+
+    def idx_column(i):
+        s = (span + i) % nspan
+        return pltpu.make_async_remote_copy(
+            idx_mid.at[s], idx_in.at[span], send_sem.at[3], recv_sem.at[3],
+            device_id=(s, group), device_id_type=MESH,
+        )
+
+    for i in range(1, nspan):
+        idx_column(i).start()
+    idx_in[span] = idx_mid[span]
 
     for c in range(8):
         slot_lane = iota((LANES, 2048), 1)
@@ -317,11 +362,14 @@
 
     loads[5].wait()
     sub = jnp.concatenate([sub_v[...], sub_v[...]], axis=0).T
-    both = whole(idx_out, idx_in, 1)
+    both = pltpu.make_async_remote_copy(
+        idx_mid.at[pl.ds(0, nspan - 1)], idx_in.at[pl.ds(0, nspan - 1)],
+        send_sem.at[3], recv_sem.at[3], device_id=column_peers[1], device_id_type=MESH,
+    )
     both.wait_send()
     both.wait_recv()
     for q in range(16):
-        at = jnp.sum(idx_in[q * 8 : q * 8 + 8, :], axis=0, keepdims=True).astype(I32)
+        at = idx_in[q].astype(I32)
         t_q = jnp.where(at == iota((LANES, LANES), 0) + 1, F32(1.0), F32(0.0))
         t_v[:, q * LANES : (q + 1) * LANES] = t_q.astype(BF16)
         tt_v[q * LANES : (q + 1) * LANES, :] = t_q.T.astype(BF16)
@@ -353,8 +401,9 @@
     gather_i = jnp.concatenate([gather_i, gather_i], axis=0)
     per_block = onehot(iota((LANES, 8 * LANES), 1) // 8 == iota((LANES, 8 * LANES), 0))
     half_lane = (iota((8 * LANES, LANES), 0) % 8) // 4 == iota((8 * LANES, LANES), 1) // 64
+    even_block = iota((8 * LANES, LANES), 0) // 8 % 2 == 0
     odd_lane = (iota((8 * LANES, LANES), 0) % 8) // 4 == iota((8 * LANES, LANES), 1) % 2
-    same = iota((8, LANES), 0) % 4 == iota((8, LANES), 1) % 4
+    same = iota((16, LANES), 0) % 4 == iota((16, LANES), 1) % 4
 
     for step in range(SSTEPS):
         beside[step, 1] = sub.astype(BF16)
@@ -366,13 +415,23 @@
         for s in sides(step):
             s.wait()
         near = mm(near_map[...], beside[step].reshape(3 * LANES, LANES))
-        near_v[...] = jnp.where(half_lane, near, F32(0.0)).astype(BF16)
-
-        @pl.loop(0, 64, unroll=8)
+        near = jnp.where(half_lane, near, F32(0.0))
+        near_v[:, :LANES] = jnp.where(even_block, near, F32(0.0)).astype(BF16)
+        near_v[:, LANES:] = jnp.where(even_block, F32(0.0), near).astype(BF16)
+
+        @pl.loop(0, 32, unroll=32)
         def _(p):
-            res = mm_nt(near_v[pl.ds(p * 16, 16), :], c_v[pl.ds(p * 256, 256), :])
-            z_v[pl.ds(p * 16, 8), :LANES] = jnp.where(same, res[:8, :LANES], F32(0.0))
-            z_v[pl.ds(p * 16 + 8, 8), :LANES] = jnp.where(same, res[8:, LANES:], F32(0.0))
+            quad = [c_v[pl.ds(p * 512 + b * LANES, LANES), :] for b in range(4)]
+            pairs = jnp.concatenate(
+                [
+                    jnp.concatenate(quad[:2], axis=1),
+                    jnp.concatenate(quad[2:], axis=1),
+                ],
+                axis=0,
+            )
+            res = mm_nt(near_v[pl.ds(p * 32, 32), :], pairs)
+            z_v[pl.ds(p * 32, 16), :LANES] = jnp.where(same, res[:16, :LANES], F32(0.0))
+            z_v[pl.ds(p * 32 + 16, 16), :LANES] = jnp.where(same, res[16:, LANES:], F32(0.0))
 
         hi, lo = split(z_v[:, :LANES])
         w = mm(jnp.concatenate([hi, lo], axis=1), gather_i)
@@ -464,13 +523,15 @@
             vmem((ndev, CAP, LANES), BF16),
             vmem((ndev, CAP, LANES), BF16),
             vmem((ndev, LANES), F32),
-            vmem((ndev, LANES), F32),
+            vmem((ngroup, nspan, LANES), F32),
+            vmem((nspan, 1, LANES), F32),
+            vmem((nspan, 1, LANES), F32),
             vmem((LANES, ndev * CAP), BF16),
             vmem((ndev * CAP, LANES), BF16),
             vmem((8 * LANES, ndev * CAP), BF16),
             vmem((8 * LANES, 8 * LANES), BF16),
             vmem((8 * LANES, 3 * LANES), BF16),
-            vmem((8 * LANES, LANES), BF16),
+            vmem((8 * LANES, 2 * LANES), BF16),
             vmem((8 * LANES, 2 * LANES), F32),
             vmem((SSTEPS, 3, LANES, LANES), BF16),
             vmem((STEPS, 1, section), F32),
@@ -478,28 +539,29 @@
             vmem((STEPS, 1, section), F32),
             vmem((STEPS, 1, section), F32),
             dma((9,)),
-            dma((3,)),
-            dma((3,)),
+            dma((4,)),
+            dma((4,)),
             dma((STEPS, 2)),
             dma((STEPS, 2)),
             dma((SSTEPS, 2)),
             dma((SSTEPS, 2)),
+            pltpu.SemaphoreType.REGULAR,
         ],
         compiler_params=pltpu.CompilerParams(
-            collective_id=0, has_side_effects=True, vmem_limit_bytes=56 << 20
+            collective_id=0, has_side_effects=True, vmem_limit_bytes=28 << 20
         ),
     )(
-        air_temp.reshape(cells, section),
-        air_vel.reshape(cells, section),
-        air_kappa.reshape(cells, section),
+        pltpu.with_memory_space_constraint(air_temp.reshape(cells, section), pltpu.HBM),
+        pltpu.with_memory_space_constraint(air_vel.reshape(cells, section), pltpu.HBM),
+        pltpu.with_memory_space_constraint(air_kappa.reshape(cells, section), pltpu.HBM),
         group_width,
-        sub_temp.T,
-        coupling,
-        neighbors.T,
+        pltpu.with_memory_space_constraint(sub_temp.T, pltpu.HBM),
+        pltpu.with_memory_space_constraint(coupling, pltpu.HBM),
+        pltpu.with_memory_space_constraint(neighbors.T, pltpu.HBM),
         iface_count,
-        iface_seg.reshape(8, LANES),
-        iface_owner.reshape(8, LANES),
-        iface_block.reshape(8, LANES),
+        pltpu.with_memory_space_constraint(iface_seg.reshape(8, LANES), pltpu.HBM),
+        pltpu.with_memory_space_constraint(iface_owner.reshape(8, LANES), pltpu.HBM),
+        pltpu.with_memory_space_constraint(iface_block.reshape(8, LANES), pltpu.HBM),
     )
     return air.reshape(1, cells, section), sub.T
 

time: 56 us -> 48.8 us (0.87)
  Pallas kernels: 50.6 us -> 45.4 us
  local copies, waits for them, and re-layouts: 3.24 us -> 1.41 us
    pallas_call x1, Pallas kernels: 50.6 us -> 45.4 us  [per_device(): pl.pallas_call(functools.partial(kernel, nspan, ngroup), out_shape=(jax.S...]
    unnamed x2, local copies, waits for them, and re-layouts: 3.24 us -> 1.41 us
where the time goes in v3:
time: 48.8 us; the launch traced here: 48.7 us
  Pallas kernels  45.4 us (93%)
  between operations  1.93 us (4%)
  local copies, waits for them, and re-layouts  1.41 us (3%)
    pallas_call x1, Pallas kernels, per_device(): pl.pallas_call(functools.partial(kernel, nspan, ngroup), out_shape=(jax.S...  45.4 us
    unnamed x2, local copies, waits for them, and re-layouts  1.41 us

profile of v3, /device:TPU:1, one launch (start us, length us, event | category | flops | bytes accessed | tf_op | source)
XLA Modules:
  0.0 48.7 jit_solution(12842887027731741327)
XLA Ops:
  1.9 45.4 %shard_map.122 = (f32[16,8192]{1,0:T(8,128)S(1)}, f32[64,128]{1,0:T(8,128)S(1)}) custom-call(f32[16,8192]{1,0:T(8,128)} %bitcast.18, f32[16,8192]{1,0:T(8,128)} %bitcast.19, f32[16,8192]{1,0:T(8,128)} %bitcast.20, s32[1]{0:T(128)S(6)} %copy.16.width_s, f32[64,128]{1,0:T(8,128)} %bitcast.21, bf16[16384,128]{1,0:T(8,128)(2,1)} %bitcast.17, s32[4,128]{1,0:T(4,128)} %bitcast.25, ...), custom_call_target="tpu_custom_call" | custom-call | tf_op jit(solution)/shard_map/pallas_call | solution.py:500
  47.3 0.8 %copy.18 = f32[1,16,8192]{2,1,0:T(8,128)} copy(f32[1,16,8192]{2,1,0:T(8,128)S(1)} %bitcast.15) | data formatting | bytes 1048576
  48.1 0.6 %copy.19 = f32[128,64]{0,1:T(8,128)} copy(f32[128,64]{0,1:T(8,128)S(1)} %bitcast.16) | data formatting | bytes 65536

commit v4 on v3

--- a/solution.py
+++ b/solution.py
@@ -70,6 +70,7 @@
     field,
     bank,
     pick,
+    pick2,
     send,
     recv,
     back,
@@ -162,13 +163,14 @@
     shift8 = jnp.where(active8, rank8.astype(I32) + group * CAP, -1)
     table = jnp.concatenate(
         [
-            place8.astype(F32),
+            jnp.where(active8, place8 % 1024, -1).astype(F32),
             key8.astype(F32),
             half8.astype(F32),
             shift8.astype(F32),
             (blk8 + 1).astype(F32),
             active8.astype(F32),
-            jnp.zeros((LANES - 48, LANES), F32),
+            (place8 // 1024).astype(F32),
+            jnp.zeros((LANES - 56, LANES), F32),
         ],
         axis=0,
     )
@@ -198,31 +200,6 @@
             z_v[k : k + 8, :LANES] = jnp.where(lane < 64, hi, pltpu.roll(lo, 64, 1))
             z_v[k : k + 8, LANES:] = jnp.where(lane < 64, pltpu.roll(hi, 64, 1), lo)
     bank[...] = z_v[...].astype(BF16)
-    key_lane = iota((LANES, 8 * LANES), 1)
-    for c in range(8):
-        rows = mm(onehot(column(1, c) == key_lane), bank[...])
-        pick[c * LANES : (c + 1) * LANES, :] = jnp.where(
-            column(2, c) == 0, rows[:, :LANES], rows[:, LANES:]
-        ).astype(BF16)
-
-    @pl.loop(0, 8)
-    def _(q):
-        slot = iota((256, LANES), 0) + q * 256
-        sel = jnp.concatenate([onehot(place8[c : c + 1, :] == slot) for c in range(8)], axis=1)
-        send[pl.ds(q * 16, 16)] = mm(sel, pick[...]).astype(BF16).reshape(16, CAP, LANES)
-
-    edge_lo[0] = air_v[0:1, :]
-    edge_hi[0] = air_v[15:16, :]
-    field[:, LANES : LANES + 8192] = air_v[...]
-
-    def pad_ends():
-        field[:, :LANES] = jnp.broadcast_to(field[:, LANES : LANES + 1], (16, LANES))
-        field[:, LANES + 8192 :] = jnp.broadcast_to(
-            field[:, LANES + 8191 : LANES + 8192], (16, LANES)
-        )
-
-    pad_ends()
-
     pl.semaphore_wait(barrier, nspan + ngroup - 2)
     for peer in row_peers[1:]:
         pl.semaphore_signal(ready, inc=1, device_id=peer, device_id_type=MESH)
@@ -239,6 +216,77 @@
     for j in range(1, ngroup):
         idx_row(j).start()
     idx_row_in[group] = idx_out[pl.ds(pl.multiple_of(group * nspan, nspan), nspan), :]
+
+    key_lane = iota((LANES, 8 * LANES), 1)
+    for c in range(8):
+        rows = mm(onehot(column(1, c) == key_lane), bank[...])
+        rows = jnp.where(column(2, c) == 0, rows[:, :LANES], rows[:, LANES:])
+        cut = slice(c * LANES, (c + 1) * LANES)
+        pick[cut, :] = rows.astype(BF16)
+        pick2[cut, :LANES] = jnp.where(column(6, c) == 0, rows, F32(0.0)).astype(BF16)
+        pick2[cut, LANES:] = jnp.where(column(6, c) == 1, rows, F32(0.0)).astype(BF16)
+
+    def send_rows(src, dst, k, s, skip_self):
+        for n, (_, g) in enumerate(row_peers):
+            copy = pltpu.make_async_remote_copy(
+                src.at[s * ngroup + g], dst.at[me], send_sem.at[k], recv_sem.at[k],
+                device_id=(s, g), device_id_type=MESH,
+            )
+            if n == 0:
+                pl.when(skip_self)(copy.start)
+            else:
+                copy.start()
+
+    place8m = jnp.where(active8, place8 % 1024, -1)
+    pl.semaphore_wait(ready, ngroup - 1)
+
+    def pack_and_send(i):
+        u = (span + i) % 8
+        slot = iota((LANES, LANES), 0) + u * LANES
+        sel = jnp.concatenate([onehot(place8m[c : c + 1, :] == slot) for c in range(8)], axis=1)
+        rows = mm(sel, pick2[...]).astype(BF16)
+        send[pl.ds(u * ngroup, ngroup)] = rows[:, :LANES].reshape(ngroup, CAP, LANES)
+        send[pl.ds((u + 8) * ngroup, ngroup)] = rows[:, LANES:].reshape(ngroup, CAP, LANES)
+        for a in range(2):
+            s = (span + i + 8 * a) % nspan
+            send_rows(send, recv, 0, s, s != span)
+
+    pl.loop(0, 4)(pack_and_send)
+    both = pltpu.make_async_remote_copy(
+        idx_row_in.at[pl.ds(0, ngroup - 1)], idx_row_in.at[pl.ds(0, ngroup - 1)],
+        send_sem.at[1], recv_sem.at[1], device_id=row_peers[1], device_id_type=MESH,
+    )
+    both.wait_send()
+    both.wait_recv()
+    total = idx_row_in[0]
+    for g in range(1, ngroup):
+        total = total + idx_row_in[g]
+    idx_mid[:, 0, :] = total
+
+    def idx_column(i):
+        s = (span + i) % nspan
+        return pltpu.make_async_remote_copy(
+            idx_mid.at[s], idx_in.at[span], send_sem.at[3], recv_sem.at[3],
+            device_id=(s, group), device_id_type=MESH,
+        )
+
+    for i in range(1, nspan):
+        idx_column(i).start()
+    idx_in[span] = idx_mid[span]
+
+    pl.loop(4, 8)(pack_and_send)
+
+    edge_lo[0] = air_v[0:1, :]
+    edge_hi[0] = air_v[15:16, :]
+    field[:, LANES : LANES + 8192] = air_v[...]
+
+    def pad_ends():
+        field[:, :LANES] = jnp.broadcast_to(field[:, LANES : LANES + 1], (16, LANES))
+        field[:, LANES + 8192 :] = jnp.broadcast_to(
+            field[:, LANES + 8191 : LANES + 8192], (16, LANES)
+        )
+
+    pad_ends()
 
     def edges(step):
         east = ((span + 1) % nspan, group)
@@ -257,55 +305,15 @@
     for e in edges(0):
         e.start()
 
-    def scatter_all(src, dst, k):
-        def to(s, g):
-            pltpu.make_async_remote_copy(
-                src.at[s * ngroup + g], dst.at[me], send_sem.at[k], recv_sem.at[k],
-                device_id=(s, g), device_id_type=MESH,
-            ).start()
-
-        for s, g in row_peers[1:]:
-            to(s, g)
-
-        @pl.loop(1, nspan)
-        def _(i):
-            s = (span + i) % nspan
-            for _, g in row_peers:
-                to(s, g)
-
     def whole(src, dst, k):
         return pltpu.make_async_remote_copy(
             src.at[pl.ds(0, ndev - 1)], dst.at[pl.ds(0, ndev - 1)], send_sem.at[k], recv_sem.at[k],
             device_id=where_is((me + 1) % ndev), device_id_type=MESH,
         )
 
-    pl.semaphore_wait(ready, ngroup - 1)
-    scatter_all(send, recv, 0)
     recv[me] = send[me]
-    both = pltpu.make_async_remote_copy(
-        idx_row_in.at[pl.ds(0, ngroup - 1)], idx_row_in.at[pl.ds(0, ngroup - 1)],
-        send_sem.at[1], recv_sem.at[1], device_id=row_peers[1], device_id_type=MESH,
-    )
-    both.wait_send()
-    both.wait_recv()
-    total = idx_row_in[0]
-    for g in range(1, ngroup):
-        total = total + idx_row_in[g]
-    idx_mid[:, 0, :] = total
-
-    def idx_column(i):
-        s = (span + i) % nspan
-        return pltpu.make_async_remote_copy(
-            idx_mid.at[s], idx_in.at[span], send_sem.at[3], recv_sem.at[3],
-            device_id=(s, group), device_id_type=MESH,
-        )
-
-    for i in range(1, nspan):
-        idx_column(i).start()
-    idx_in[span] = idx_mid[span]
-
     for c in range(8):
-        slot_lane = iota((LANES, 2048), 1)
+        slot_lane = iota((LANES, 1024), 1)
         pt_v[c * LANES : (c + 1) * LANES, :] = onehot(column(0, c) == slot_lane)
 
     @pl.loop(0, 8)
@@ -441,8 +449,15 @@
 
     hi = sub.astype(BF16).astype(F32)
     pair = jnp.where(lane2 < 64, hi, sub - hi).astype(BF16)
-    back[...] = mm(tt_v[...], pair).astype(BF16).reshape(ndev, CAP, LANES)
-    scatter_all(back, got, 2)
+    @pl.loop(0, 8)
+    def _(i):
+        q = (span // 2 + i) % 8
+        rows = mm(tt_v[pl.ds(q * 256, 256), :], pair)
+        back[pl.ds(q * 16, 16)] = rows.astype(BF16).reshape(16, CAP, LANES)
+        for a in range(2):
+            s = q * 2 + (span + a) % 2
+            send_rows(back, got, 2, s, s != span)
+
     got[me] = back[me]
     sub_o[...] = sub.T[:64, :]
     advance(3)
@@ -450,9 +465,13 @@
     both.wait_send()
     both.wait_recv()
 
+    got2 = jnp.concatenate(
+        [got[:64].reshape(1024, LANES), got[64:].reshape(1024, LANES)], axis=1
+    )
     for c in range(8):
         rows = slice(c * LANES, (c + 1) * LANES)
-        surf = mm(pt_v[rows, :], got[...].reshape(2048, LANES))
+        surf = mm(pt_v[rows, :], got2)
+        surf = jnp.where(column(6, c) == 0, surf[:, :LANES], surf[:, LANES:])
         gap = surf - pick[rows, :].astype(F32)
         gap = RELEASE * (gap + pltpu.roll(gap, 64, 1))
         keep = jnp.logical_and(column(5, c) == 1, column(2, c) == lane2 // 64)
@@ -518,6 +537,7 @@
             vmem((cells, section + 2 * LANES), F32),
             vmem((8 * LANES, 2 * LANES), BF16),
             vmem((8 * LANES, LANES), BF16),
+            vmem((8 * LANES, 2 * LANES), BF16),
             vmem((ndev, CAP, LANES), BF16),
             vmem((ndev, CAP, LANES), BF16),
             vmem((ndev, CAP, LANES), BF16),
@@ -528,7 +548,7 @@
             vmem((nspan, 1, LANES), F32),
             vmem((LANES, ndev * CAP), BF16),
             vmem((ndev * CAP, LANES), BF16),
-            vmem((8 * LANES, ndev * CAP), BF16),
+            vmem((8 * LANES, ndev * CAP // 2), BF16),
             vmem((8 * LANES, 8 * LANES), BF16),
             vmem((8 * LANES, 3 * LANES), BF16),
             vmem((8 * LANES, 2 * LANES), BF16),

time: 48.8 us -> 47.7 us (0.977)
  Pallas kernels: 45.4 us -> 44.2 us
    pallas_call x1, Pallas kernels: 45.4 us -> 44.2 us  [per_device(): pl.pallas_call(functools.partial(kernel, nspan, ngroup), out_shape=(jax.S...]
where the time goes in v4:
time: 47.7 us; the launch traced here: 47.5 us
  Pallas kernels  44.2 us (93%)
  between operations  1.93 us (4%)
  local copies, waits for them, and re-layouts  1.41 us (3%)
    pallas_call x1, Pallas kernels, per_device(): pl.pallas_call(functools.partial(kernel, nspan, ngroup), out_shape=(jax.S...  44.2 us
    unnamed x2, local copies, waits for them, and re-layouts  1.41 us

profile of v4, /device:TPU:1, one launch (start us, length us, event | category | flops | bytes accessed | tf_op | source)
XLA Modules:
  0.0 47.5 jit_solution(4101762092825514490)
XLA Ops:
  1.9 44.2 %shard_map.122 = (f32[16,8192]{1,0:T(8,128)S(1)}, f32[64,128]{1,0:T(8,128)S(1)}) custom-call(f32[16,8192]{1,0:T(8,128)} %bitcast.18, f32[16,8192]{1,0:T(8,128)} %bitcast.19, f32[16,8192]{1,0:T(8,128)} %bitcast.20, s32[1]{0:T(128)S(6)} %copy.16.width_s, f32[64,128]{1,0:T(8,128)} %bitcast.21, bf16[16384,128]{1,0:T(8,128)(2,1)} %bitcast.17, s32[4,128]{1,0:T(4,128)} %bitcast.25, ...), custom_call_target="tpu_custom_call" | custom-call | tf_op jit(solution)/shard_map/pallas_call | solution.py:519
  46.1 0.8 %copy.18 = f32[1,16,8192]{2,1,0:T(8,128)} copy(f32[1,16,8192]{2,1,0:T(8,128)S(1)} %bitcast.15) | data formatting | bytes 1048576
  46.9 0.6 %copy.19 = f32[128,64]{0,1:T(8,128)} copy(f32[128,64]{0,1:T(8,128)S(1)} %bitcast.16) | data formatting | bytes 65536

commit v5 on v4

--- a/solution.py
+++ b/solution.py
@@ -123,7 +123,8 @@
         )
     ):
         copy = pltpu.make_async_copy(src, dst, in_sem.at[k])
-        copy.start()
+        if k < 6:
+            copy.start()
         loads.append(copy)
 
     barrier = pltpu.get_barrier_semaphore()
@@ -191,6 +192,8 @@
     idx_out[...] = mm(owners, slots)
 
     loads[3].wait()
+    for k in range(6, 9):
+        loads[k].start()
     for line in range(2):
         for j in range(64):
             k = (line * 64 + j) * 8
@@ -414,7 +417,7 @@
     same = iota((16, LANES), 0) % 4 == iota((16, LANES), 1) % 4
 
     for step in range(SSTEPS):
-        beside[step, 1] = sub.astype(BF16)
+        beside[step, 1] = jnp.where(lane2[:64] < 64, sub[:64], sub[64:]).astype(BF16)
         for s in sides(step):
             s.start()
         advance(step + 1)
@@ -422,7 +425,12 @@
             loads[8].wait()
         for s in sides(step):
             s.wait()
-        near = mm(near_map[...], beside[step].reshape(3 * LANES, LANES))
+        full = []
+        for n in range(3):
+            x = beside[step, n].astype(F32)
+            y = pltpu.roll(x, 64, 1)
+            full += [jnp.where(lane2[:64] < 64, x, y), jnp.where(lane2[:64] < 64, y, x)]
+        near = mm(near_map[...], jnp.concatenate(full, axis=0).astype(BF16))
         near = jnp.where(half_lane, near, F32(0.0))
         near_v[:, :LANES] = jnp.where(even_block, near, F32(0.0)).astype(BF16)
         near_v[:, LANES:] = jnp.where(even_block, F32(0.0), near).astype(BF16)
@@ -553,7 +561,7 @@
             vmem((8 * LANES, 3 * LANES), BF16),
             vmem((8 * LANES, 2 * LANES), BF16),
             vmem((8 * LANES, 2 * LANES), F32),
-            vmem((SSTEPS, 3, LANES, LANES), BF16),
+            vmem((SSTEPS, 3, LANES // 2, LANES), BF16),
             vmem((STEPS, 1, section), F32),
             vmem((STEPS, 1, section), F32),
             vmem((STEPS, 1, section), F32),

time: 47.7 us -> 47.4 us (level)
  no operation moved by 1% of the time
where the time goes in v5:
time: 47.4 us; the launch traced here: 47.3 us
  Pallas kernels  43.9 us (93%)
  between operations  1.93 us (4%)
  local copies, waits for them, and re-layouts  1.41 us (3%)
    pallas_call x1, Pallas kernels, per_device(): pl.pallas_call(functools.partial(kernel, nspan, ngroup), out_shape=(jax.S...  43.9 us
    unnamed x2, local copies, waits for them, and re-layouts  1.41 us

profile of v5, /device:TPU:1, one launch (start us, length us, event | category | flops | bytes accessed | tf_op | source)
XLA Modules:
  0.0 47.3 jit_solution(4568228931423146266)
XLA Ops:
  1.9 43.9 %shard_map.122 = (f32[16,8192]{1,0:T(8,128)S(1)}, f32[64,128]{1,0:T(8,128)S(1)}) custom-call(f32[16,8192]{1,0:T(8,128)} %bitcast.18, f32[16,8192]{1,0:T(8,128)} %bitcast.19, f32[16,8192]{1,0:T(8,128)} %bitcast.20, s32[1]{0:T(128)S(6)} %copy.16.width_s, f32[64,128]{1,0:T(8,128)} %bitcast.21, bf16[16384,128]{1,0:T(8,128)(2,1)} %bitcast.17, s32[4,128]{1,0:T(4,128)} %bitcast.25, ...), custom_call_target="tpu_custom_call" | custom-call | tf_op jit(solution)/shard_map/pallas_call | solution.py:527
  45.9 0.8 %copy.18 = f32[1,16,8192]{2,1,0:T(8,128)} copy(f32[1,16,8192]{2,1,0:T(8,128)S(1)} %bitcast.15) | data formatting | bytes 1048576
  46.7 0.6 %copy.19 = f32[128,64]{0,1:T(8,128)} copy(f32[128,64]{0,1:T(8,128)S(1)} %bitcast.16) | data formatting | bytes 65536
